TPU v7x, 128 devices: a whole 4x4x4 slice. The times are simulated.
128 devices in a mesh: user: 8 (over y, core), item: 16 (over x, z).
Axes of the slice: x: 4, y: 4, z: 4, core: 2. Of those that a mesh axis runs over, the one named last changes fastest.
Arguments:
- item_factor: float32 [32768, 256], P(('item', 'user')), may hold values from -36 to 36
- context_factor: float32 [4096, 256], replicated, may hold values from -6 to 6
- tile_count: int32 [8, 16], P('user', 'item'), may hold values from 16 to 128, as said below
- tile_rows: int32 [8, 16, 128], P('user', 'item'), may hold values from 0 to 63
- tile_cols: int32 [8, 16, 128], P('user', 'item'), may hold values from 0 to 31
- tile_ctx: int32 [8, 16, 128], P('user', 'item'), may hold values from 0 to 63
- nz_offsets: int32 [8, 16, 3, 128, 512], P('user', 'item'), may hold values from 0 to 63
- nz_values: float32 [8, 16, 128, 512], P('user', 'item'), may hold values from -6 to 6
Outputs:
- user_factor: float32 [32768, 256], P(('user', 'item'))
- new_items: float32 [32768, 256], P(('item', 'user'))
Inputs may be any that keep to these rules, and one draw needn't show every extreme that they name: `tile_count`: some device has all 128 tiles live; the others 128, half, a quarter or an eighth of them.
All inputs are finite; a program needn't handle non-finite values.
Results may differ from a plain program's by a relative error of at most 0.0066.
Values may be sent and summed in bfloat16 or wider, within the bound.
A program may use at most 128 MiB of HBM per device.

v0:
```python
import jax
import jax.numpy as jnp
from jax import lax
from jax.sharding import PartitionSpec as P

TILE = 64
USR_DEV = 256
ITM_DEV = 256


def solve_rows(right_side, gram):
    lower_factor = jnp.linalg.cholesky(gram)
    partway = lax.linalg.triangular_solve(
        lower_factor, right_side, left_side=False, lower=True, transpose_a=True
    )
    return lax.linalg.triangular_solve(
        lower_factor, partway, left_side=False, lower=True, transpose_a=False
    )


def mttkrp(
    live_count,
    target_ids,
    target_offsets,
    target_tiles,
    source_tiles,
    source_ids,
    source_offsets,
    context_tiles,
    context_ids,
    context_offsets,
    values,
):
    rank_width = source_tiles.shape[2]
    per_step = 8
    steps_count = (live_count + per_step - 1) // per_step
    positions = jnp.arange(TILE, dtype=jnp.int32)

    def one_hot(offsets):
        return (offsets[..., None] == positions).astype(jnp.bfloat16)

    def advance(step_index, totals):
        first = step_index * per_step
        alive = (first + jnp.arange(per_step, dtype=jnp.int32) < live_count).astype(jnp.float32)
        step_targets = lax.dynamic_slice_in_dim(target_ids, first, per_step, 0)
        step_sources = lax.dynamic_slice_in_dim(source_ids, first, per_step, 0)
        step_contexts = lax.dynamic_slice_in_dim(context_ids, first, per_step, 0)
        step_values = lax.dynamic_slice_in_dim(values, first, per_step, 0) * alive[:, None]
        source_rows = jnp.einsum(
            "bnt,btr->bnr",
            one_hot(lax.dynamic_slice_in_dim(source_offsets, first, per_step, 0)),
            source_tiles[step_sources],
            preferred_element_type=jnp.float32,
        )
        context_rows = jnp.einsum(
            "bnt,btr->bnr",
            one_hot(lax.dynamic_slice_in_dim(context_offsets, first, per_step, 0)),
            context_tiles[step_contexts],
            preferred_element_type=jnp.float32,
        )
        terms = (step_values[:, :, None] * source_rows * context_rows).astype(jnp.bfloat16)
        placed = jnp.einsum(
            "bnt,bnr->btr",
            one_hot(lax.dynamic_slice_in_dim(target_offsets, first, per_step, 0)),
            terms,
            preferred_element_type=jnp.float32,
        )
        return totals.at[step_targets].add(placed)

    totals = jnp.zeros((target_tiles, TILE, rank_width), jnp.float32)
    totals = lax.fori_loop(0, steps_count, advance, totals)
    return totals.reshape(target_tiles * TILE, rank_width)


def local(
    item_factor, context_factor, tile_count, tile_rows, tile_cols, tile_ctx, nz_offsets, nz_values
):
    highest = lax.Precision.HIGHEST
    rank_width = item_factor.shape[1]
    user_count = lax.axis_size("user")
    item_count = lax.axis_size("item")
    user_block = USR_DEV * item_count
    item_block = ITM_DEV * user_count
    users_total = user_block * user_count
    items_total = item_block * item_count
    live_count = tile_count[0, 0]
    row_ids = tile_rows[0, 0]
    col_ids = tile_cols[0, 0]
    ctx_ids = tile_ctx[0, 0]
    offsets = nz_offsets[0, 0]
    values = nz_values[0, 0]
    context_tiles = context_factor.astype(jnp.bfloat16).reshape(-1, TILE, rank_width)
    context_gram = jnp.dot(
        context_factor.T, context_factor, precision=highest, preferred_element_type=jnp.float32
    )
    item_gram = lax.psum(
        jnp.dot(item_factor.T, item_factor, precision=highest, preferred_element_type=jnp.float32),
        ("user", "item"),
    )
    item_local = lax.all_gather(item_factor.astype(jnp.bfloat16), "user", axis=0, tiled=True)
    partial_users = mttkrp(
        live_count,
        row_ids,
        offsets[0],
        user_block // TILE,
        item_local.reshape(-1, TILE, rank_width),
        col_ids,
        offsets[1],
        context_tiles,
        ctx_ids,
        offsets[2],
        values,
    )
    user_system = item_gram * context_gram
    owned_sum = lax.psum_scatter(partial_users, "item", scatter_dimension=0, tiled=True)
    raw_rows = solve_rows(owned_sum, user_system)
    raw_gram = lax.psum(
        jnp.dot(raw_rows.T, raw_rows, precision=highest, preferred_element_type=jnp.float32),
        ("user", "item"),
    )
    column_scale = jnp.sqrt(users_total / (jnp.diagonal(raw_gram) + 1e-06))
    owned_users = raw_rows * column_scale
    user_local = lax.all_gather(owned_users.astype(jnp.bfloat16), "item", axis=0, tiled=True)
    user_gram = raw_gram * column_scale[:, None] * column_scale[None, :]
    partial_items = mttkrp(
        live_count,
        col_ids,
        offsets[1],
        item_block // TILE,
        user_local.reshape(-1, TILE, rank_width),
        row_ids,
        offsets[0],
        context_tiles,
        ctx_ids,
        offsets[2],
        values,
    )
    owned_items = lax.psum_scatter(partial_items, "user", scatter_dimension=0, tiled=True)
    item_raw = solve_rows(owned_items, user_gram * context_gram)
    item_squares = lax.psum(jnp.sum(item_raw * item_raw, axis=0), ("user", "item"))
    new_items = item_raw * jnp.sqrt(items_total / (item_squares + 1e-06))
    return (owned_users, new_items)


def solution(mesh):
    in_specs = (
        P(("item", "user"), None),
        P(),
        P("user", "item"),
        P("user", "item", None),
        P("user", "item", None),
        P("user", "item", None),
        P("user", "item", None, None, None),
        P("user", "item", None, None),
    )
    out_specs = (P(("user", "item"), None), P(("item", "user"), None))
    return jax.shard_map(local, mesh=mesh, in_specs=in_specs, out_specs=out_specs, check_vma=False)
```

profile of v0, /device:TPU:1, one launch (start us, length us, event | category | flops | bytes accessed | tf_op | source)
XLA Modules:
  0.0 921.8 jit_solution(2475890599702103652)
XLA Ops:
  17.2 20.4 %all-gather.3.cloned.1.call-done = bf16[2048,256]{1,0:T(8,128)(2,1)} async-done(((bf16[256,256]{1,0:T(8,128)(2,1)}), bf16[2048,256]{1,0:T(8,128)(2,1)}) %all-gather.3.cloned.1.call-update) | async-done | bytes 1048592 | tf_op jit(solution)/shard_map/all_gather | solution.py:100
  40.1 115.4 %while.32 = (s32[]{:T(128)}, f32[64,64,256]{2,1,0:T(8,128)}, s32[]{:T(128)}, s32[128]{0:T(128)S(1)}, s32[128,512]{1,0:T(8,128)}, /*index=5*/f32[128,512]{1,0:T(8...) while((s32[]{:T(128)}, f32[64,64,256]{2,1,0:T(8,128)}, ...), condition=%wide.region_7.9_spmd.clone.clone, body=%wide.region_5.8_spmd.clone.clone.sunk | while | flops 406722656 | bytes 12264079 | solution.py:71
  48.3 3.6 fusion.83
  134.8 3.6 fusion.83
  149.2 3.6 fusion.83
  156.2 3.7 all-reduce.4.cloned.1.call-done
  159.9 10.2 %fusion.46 = (f32[256,256]{0,1:T(8,128)S(1)}, f32[256,256]{0,1:T(8,128)S(1)}) fusion(f32[256,256]{0,1:T(8,128)} %all-reduce.4.cloned.1.call-done, f32[4096,256]{1,0:T(8,128)} %param.18), kind=kOutput, calls=%fused_computation.122 | convolution fusion | flops 3221291008 | bytes 4980736 | tf_op jit(solution)/shard_map/dot_general | solution.py:93
  170.3 11.7 %cholesky.130 = f32[128,128]{1,0:T(8,128)S(1)} custom-call(f32[128,128]{1,0:T(8,128)S(1)} %cholesky.194), custom_call_target="Cholesky" | custom-call | tf_op jit(solution)/shard_map/jit(cholesky)/cholesky | solution.py:12
  182.0 9.9 %custom-call.19 = f32[1,128,128]{1,2,0:T(8,128)S(1)} custom-call(f32[1,128,128]{2,1,0:T(8,128)S(1)} %get-tuple-element.432), custom_call_target="InvertDiagBlocksLowerTriangular" | custom-call | tf_op jit(solution)/shard_map/jit(cholesky)/cholesky | solution.py:12
  192.5 11.7 %cholesky.147 = f32[128,128]{1,0:T(8,128)S(1)} custom-call(f32[128,128]{1,0:T(8,128)S(1)} %convolution_subtract_fusion.5), custom_call_target="Cholesky" | custom-call | tf_op jit(solution)/shard_map/jit(cholesky)/cholesky | solution.py:12
  206.2 3.9 while.34
  210.2 19.7 %custom-call.20 = f32[2,128,128]{1,2,0:T(8,128)S(1)} custom-call(f32[2,128,128]{2,1,0:T(8,128)S(1)} %get-tuple-element.319), custom_call_target="InvertDiagBlocksLowerTriangular" | custom-call | tf_op jit(solution)/shard_map/triangular_solve/custom-call.0 | solution.py:13
  229.8 116.2 %reduce-scatter.3.cloned.1.call-done = f32[256,256]{1,0:T(8,128)} async-done(((f32[4096,256]{1,0:T(8,128)}), f32[256,256]{1,0:T(8,128)}) %reduce-scatter.3.cloned.1.call-update) | async-done | bytes 262160 | tf_op jit(solution)/shard_map/reduce_scatter | solution.py:115
  351.0 142.3 %all-reduce.6.cloned.1.call-done = f32[256,256]{0,1:T(8,128)} async-done(((f32[256,256]{0,1:T(8,128)}), f32[256,256]{0,1:T(8,128)}) %all-reduce.6.cloned.1.call-update) | async-done | bytes 262160 | tf_op jit(solution)/shard_map/psum | solution.py:117
  497.8 44.1 %all-gather.5.cloned.1.call-done = bf16[4096,256]{0,1:T(8,128)(2,1)} async-done(((bf16[256,256]{0,1:T(8,128)(2,1)}), bf16[4096,256]{0,1:T(8,128)(2,1)}) %all-gather.5.cloned.1.call-update) | async-done | bytes 2097168 | tf_op jit(solution)/shard_map/all_gather | solution.py:123
  541.9 4.1 copy.25
  546.3 118.1 %while.33 = (s32[]{:T(128)}, f32[32,64,256]{2,1,0:T(8,128)S(1)}, s32[]{:T(128)}, s32[128]{0:T(128)S(1)}, s32[128,512]{1,0:T(8,128)}, /*index=5*/f32[128,512]{1,0...) while((s32[]{:T(128)}, f32[32,64,256]{2,1,0:T(8,128)S(1)}, ...), condition=%wide.region_12.16_spmd.clone.clone, body=%wide.region_10.0_spmd.clone.clone.sunk | while | flops 406722656 | bytes 12264079 | solution.py:71
  666.8 11.7 %cholesky.164 = f32[128,128]{1,0:T(8,128)S(1)} custom-call(f32[128,128]{1,0:T(8,128)S(1)} %cholesky.197), custom_call_target="Cholesky" | custom-call | tf_op jit(solution)/shard_map/jit(cholesky)/cholesky | solution.py:12
  678.5 9.8 %custom-call.22 = f32[1,128,128]{1,2,0:T(8,128)S(1)} custom-call(f32[1,128,128]{2,1,0:T(8,128)S(1)} %get-tuple-element.428), custom_call_target="InvertDiagBlocksLowerTriangular" | custom-call | tf_op jit(solution)/shard_map/jit(cholesky)/cholesky | solution.py:12
  688.8 11.7 %cholesky.181 = f32[128,128]{1,0:T(8,128)S(1)} custom-call(f32[128,128]{1,0:T(8,128)S(1)} %convolution_subtract_fusion.4), custom_call_target="Cholesky" | custom-call | tf_op jit(solution)/shard_map/jit(cholesky)/cholesky | solution.py:12
  703.1 4.1 while.35
  707.2 19.7 %custom-call.23 = f32[2,128,128]{1,2,0:T(8,128)S(1)} custom-call(f32[2,128,128]{2,1,0:T(8,128)S(1)} %get-tuple-element.321), custom_call_target="InvertDiagBlocksLowerTriangular" | custom-call | tf_op jit(solution)/shard_map/triangular_solve/custom-call.0 | solution.py:13
  726.9 87.1 %reduce-scatter.5.cloned.1.call-done = f32[256,256]{1,0:T(8,128)} async-done(((f32[2048,256]{1,0:T(8,128)}), f32[256,256]{1,0:T(8,128)}) %reduce-scatter.5.cloned.1.call-update) | async-done | bytes 262160 | tf_op jit(solution)/shard_map/reduce_scatter | solution.py:138
  817.9 95.6 %psum.23 = f32[256]{0:T(256)S(1)} all-reduce(f32[256]{0:T(256)S(1)} %multiply_reduce_fusion), channel_id=1, replica_groups=mesh['user'=8,'item'=16] {'user','item'}, use_global_device_ids=true, to_apply=%region_15.19 | all-reduce | flops 256 | bytes 2048 | tf_op jit(solution)/shard_map/psum | solution.py:140
  (296 shorter events, 261.1 us)
Async XLA Ops:
  8.0 29.6 %all-gather.3.cloned.1.call-start = ((), (), s32[]{:S(2)}) async-start(), calls=%async_computation.3 | async-start | bytes 1179648 | tf_op jit(solution)/shard_map/all_gather | solution.py:100
  9.7 150.2 %all-reduce.4.cloned.1.call-start = ((), (), s32[]{:S(2)}) async-start(), calls=%async_computation.2 | async-start | bytes 524288 | tf_op jit(solution)/shard_map/psum | solution.py:96
  12.1 334.0 %reduce-scatter.3.cloned.1.call-start = ((), (), s32[]{:S(2)}) async-start(), calls=%async_computation.4 | async-start | bytes 4456448 | tf_op jit(solution)/shard_map/reduce_scatter | solution.py:115
  14.8 25.3 %copy-start.4 = (s32[1,1,128]{2,1,0:T(1,128)S(1)}, s32[1,1,128]{2,1,0:T(1,128)}, u32[]{:S(2)}) copy-start(s32[1,1,128]{2,1,0:T(1,128)} %param.22) | copy-start | bytes 1540
  14.8 25.3 %copy-start.5 = (s32[1,1,128]{2,1,0:T(1,128)S(1)}, s32[1,1,128]{2,1,0:T(1,128)}, u32[]{:S(2)}) copy-start(s32[1,1,128]{2,1,0:T(1,128)} %param.20) | copy-start | bytes 1540
  14.8 25.3 %copy-start.6 = (s32[1,1,128]{2,1,0:T(1,128)S(1)}, s32[1,1,128]{2,1,0:T(1,128)}, u32[]{:S(2)}) copy-start(s32[1,1,128]{2,1,0:T(1,128)} %param.21) | copy-start | bytes 1540
  155.5 0.7 copy-start.3
  155.5 14.6 %copy-start.1 = (bf16[64,64,256]{2,1,0:T(8,128)(2,1)}, bf16[64,64,256]{2,1,0:T(8,128)(2,1)S(1)}, u32[]{:S(2)}) copy-start(bf16[64,64,256]{2,1,0:T(8,128)(2,1)S(1)} %get-tuple-element.818) | copy-start | bytes 6291460
  155.5 337.8 %all-reduce.6.cloned.1.call-start = ((), (), s32[]{:S(2)}) async-start(), calls=%async_computation.5 | async-start | bytes 524288 | tf_op jit(solution)/shard_map/psum | solution.py:117
  350.9 191.0 %all-gather.5.cloned.1.call-start = ((), (), s32[]{:S(2)}) async-start(), calls=%async_computation.6 | async-start | bytes 2228224 | tf_op jit(solution)/shard_map/all_gather | solution.py:123
  497.8 316.2 %reduce-scatter.5.cloned.1.call-start = ((), (), s32[]{:S(2)}) async-start(), calls=%async_computation.7 | async-start | bytes 2359296 | tf_op jit(solution)/shard_map/reduce_scatter | solution.py:138
  546.3 119.5 %copy-start.2 = (f32[256,256]{0,1:T(8,128)S(1)}, f32[256,256]{0,1:T(8,128)}, u32[]{:S(2)}) copy-start(f32[256,256]{0,1:T(8,128)} %get-tuple-element.409) | copy-start | bytes 786436
  664.3 1.4 copy-start
Sparse Core Ops, SparseCore 0:
  10.5 27.0 all-gather.2
  155.6 190.4 reduce-scatter.2
  497.9 43.9 all-gather.4
  665.8 148.1 reduce-scatter.4
Sparse Core Ops, SparseCore 1:
  14.9 144.9 all-reduce.3
  351.0 142.2 all-reduce.5
where the time goes:
time: 936 us; the launch traced here: 922 us
  waiting for transfers between devices  414 us (44%)
  other arithmetic  170 us (18%)
  matrix products  122 us (13%)
  local copies, waits for them, and re-layouts  99 us (11%)
  blocking collectives  95.6 us (10%)
  between operations  18.9 us (2%)
    psum x1, waiting for transfers between devices, local(): lax.psum(jnp.dot(raw_rows.T, raw_rows, precision=highest, preferred_eleme...  142 us
    reduce_scatter x1, waiting for transfers between devices, local(): lax.psum_scatter(partial_users, 'item', scatter_dimension=0, tiled=True)  116 us
    psum x1, blocking collectives, local(): lax.psum(jnp.sum(item_raw * item_raw, axis=0), ('user', 'item'))  95.6 us
    reduce_scatter x1, waiting for transfers between devices, local(): lax.psum_scatter(partial_items, 'user', scatter_dimension=0, tiled=True)  87.1 us
    another operation x13, other arithmetic, solve_rows(): lower_factor = jnp.linalg.cholesky(gram)  68.7 us
    dot_general x16, matrix products, advance(): jnp.einsum('bnt,bnr->btr', one_hot(lax.dynamic_slice_in_dim(target_offset...  57.1 us
    all_gather x1, waiting for transfers between devices, local(): lax.all_gather(owned_users.astype(jnp.bfloat16), 'item', axis=0, tiled=True)  44.1 us
    dot_general x16, matrix products, advance(): jnp.einsum('bnt,btr->bnr', one_hot(lax.dynamic_slice_in_dim(source_offset...  43.4 us
  transfers between devices with their start and end apart: 6, of which 6 were waited for; matrix products, arithmetic and copies ran while one was open for 27% of the time, Pallas kernels for 0%

commit v1 on v0

--- a/solution.py
+++ b/solution.py
@@ -75,6 +75,12 @@
 def local(
     item_factor, context_factor, tile_count, tile_rows, tile_cols, tile_ctx, nz_offsets, nz_values
 ):
+
+    def write_sums_all(panel, shard_axis, bus_axis):
+        f_next = lax.psum(panel, shard_axis)
+        res = lax.psum(f_next, bus_axis)
+        return res
+
     highest = lax.Precision.HIGHEST
     rank_width = item_factor.shape[1]
     user_count = lax.axis_size("user")
@@ -137,7 +143,7 @@
     )
     owned_items = lax.psum_scatter(partial_items, "user", scatter_dimension=0, tiled=True)
     item_raw = solve_rows(owned_items, user_gram * context_gram)
-    item_squares = lax.psum(jnp.sum(item_raw * item_raw, axis=0), ("user", "item"))
+    item_squares = write_sums_all(jnp.sum(item_raw * item_raw, axis=0), "user", "item")
     new_items = item_raw * jnp.sqrt(items_total / (item_squares + 1e-06))
     return (owned_users, new_items)
 

time: 936 us -> 920 us (0.983)
  the two profiles are of different devices: /device:TPU:1 before, /device:TPU:0 now
where the time goes in v1:
time: 920 us; the launch traced here: 906 us
  waiting for transfers between devices  533 us (58%)
  other arithmetic  142 us (15%)
  blocking collectives  77.6 us (8%)
  matrix products  72.2 us (8%)
  local copies, waits for them, and re-layouts  60.7 us (7%)
  between operations  18.9 us (2%)
    reduce_scatter x1, waiting for transfers between devices, local(): lax.psum_scatter(partial_items, 'user', scatter_dimension=0, tiled=True)  148 us
    psum x1, waiting for transfers between devices, local(): lax.psum(jnp.dot(raw_rows.T, raw_rows, precision=highest, preferred_eleme...  141 us
    reduce_scatter x1, waiting for transfers between devices, local(): lax.psum_scatter(partial_users, 'item', scatter_dimension=0, tiled=True)  118 us
    another operation x13, other arithmetic, solve_rows(): lower_factor = jnp.linalg.cholesky(gram)  68.7 us
    psum x1, blocking collectives, write_sums_all(): res = lax.psum(f_next, bus_axis)  64.9 us
    psum x1, waiting for transfers between devices, local(): lax.psum(jnp.dot(item_factor.T, item_factor, precision=highest, preferred...  61.9 us
    all_gather x1, waiting for transfers between devices, local(): lax.all_gather(owned_users.astype(jnp.bfloat16), 'item', axis=0, tiled=True)  44.9 us
    another operation x5, other arithmetic, solve_rows(): lax.linalg.triangular_solve(lower_factor, right_side, left_side=False, lo...  39.4 us
  transfers between devices with their start and end apart: 6, of which 6 were waited for; matrix products, arithmetic and copies ran while one was open for 22% of the time, Pallas kernels for 0%

profile of v1, /device:TPU:0, one launch (start us, length us, event | category | flops | bytes accessed | tf_op | source)
XLA Modules:
  0.0 906.1 jit_solution(11333845710198201042)
XLA Ops:
  17.2 19.2 %all-gather.3.cloned.1.call-done = bf16[2048,256]{1,0:T(8,128)(2,1)} async-done(((bf16[256,256]{1,0:T(8,128)(2,1)}), bf16[2048,256]{1,0:T(8,128)(2,1)}) %all-gather.3.cloned.1.call-update) | async-done | bytes 1048592 | tf_op jit(solution)/shard_map/all_gather | solution.py:106
  38.9 57.7 %while.32 = (s32[]{:T(128)}, f32[64,64,256]{2,1,0:T(8,128)}, s32[]{:T(128)}, s32[128]{0:T(128)S(1)}, s32[128,512]{1,0:T(8,128)}, /*index=5*/f32[128,512]{1,0:T(8...) while((s32[]{:T(128)}, f32[64,64,256]{2,1,0:T(8,128)}, ...), condition=%wide.region_7.9_spmd.clone.clone, body=%wide.region_5.8_spmd.clone.clone.sunk | while | flops 406722656 | bytes 12264079 | solution.py:71
  47.1 3.6 fusion.83
  61.5 3.6 fusion.83
  97.3 61.9 %all-reduce.4.cloned.1.call-done = f32[256,256]{0,1:T(8,128)} async-done(((f32[256,256]{0,1:T(8,128)}), f32[256,256]{0,1:T(8,128)}) %all-reduce.4.cloned.1.call-update) | async-done | bytes 262160 | tf_op jit(solution)/shard_map/psum | solution.py:102
  159.2 10.2 %fusion.46 = (f32[256,256]{0,1:T(8,128)S(1)}, f32[256,256]{0,1:T(8,128)S(1)}) fusion(f32[256,256]{0,1:T(8,128)} %all-reduce.4.cloned.1.call-done, f32[4096,256]{1,0:T(8,128)} %param.18), kind=kOutput, calls=%fused_computation.122 | convolution fusion | flops 3221291008 | bytes 4980736 | tf_op jit(solution)/shard_map/dot_general | solution.py:99
  169.6 11.7 %cholesky.130 = f32[128,128]{1,0:T(8,128)S(1)} custom-call(f32[128,128]{1,0:T(8,128)S(1)} %cholesky.194), custom_call_target="Cholesky" | custom-call | tf_op jit(solution)/shard_map/jit(cholesky)/cholesky | solution.py:12
  181.4 9.9 %custom-call.19 = f32[1,128,128]{1,2,0:T(8,128)S(1)} custom-call(f32[1,128,128]{2,1,0:T(8,128)S(1)} %get-tuple-element.432), custom_call_target="InvertDiagBlocksLowerTriangular" | custom-call | tf_op jit(solution)/shard_map/jit(cholesky)/cholesky | solution.py:12
  191.8 11.7 %cholesky.147 = f32[128,128]{1,0:T(8,128)S(1)} custom-call(f32[128,128]{1,0:T(8,128)S(1)} %convolution_subtract_fusion.5), custom_call_target="Cholesky" | custom-call | tf_op jit(solution)/shard_map/jit(cholesky)/cholesky | solution.py:12
  205.6 3.9 while.34
  209.5 19.7 %custom-call.20 = f32[2,128,128]{1,2,0:T(8,128)S(1)} custom-call(f32[2,128,128]{2,1,0:T(8,128)S(1)} %get-tuple-element.319), custom_call_target="InvertDiagBlocksLowerTriangular" | custom-call | tf_op jit(solution)/shard_map/triangular_solve/custom-call.0 | solution.py:13
  229.2 117.8 %reduce-scatter.3.cloned.1.call-done = f32[256,256]{1,0:T(8,128)} async-done(((f32[4096,256]{1,0:T(8,128)}), f32[256,256]{1,0:T(8,128)}) %reduce-scatter.3.cloned.1.call-update) | async-done | bytes 262160 | tf_op jit(solution)/shard_map/reduce_scatter | solution.py:121
  351.9 140.8 %all-reduce.6.cloned.1.call-done = f32[256,256]{0,1:T(8,128)} async-done(((f32[256,256]{0,1:T(8,128)}), f32[256,256]{0,1:T(8,128)}) %all-reduce.6.cloned.1.call-update) | async-done | bytes 262160 | tf_op jit(solution)/shard_map/psum | solution.py:123
  497.2 44.9 %all-gather.5.cloned.1.call-done = bf16[4096,256]{0,1:T(8,128)(2,1)} async-done(((bf16[256,256]{0,1:T(8,128)(2,1)}), bf16[4096,256]{0,1:T(8,128)(2,1)}) %all-gather.5.cloned.1.call-update) | async-done | bytes 2097168 | tf_op jit(solution)/shard_map/all_gather | solution.py:129
  542.1 4.1 copy.25
  546.4 59.1 %while.33 = (s32[]{:T(128)}, f32[32,64,256]{2,1,0:T(8,128)S(1)}, s32[]{:T(128)}, s32[128]{0:T(128)S(1)}, s32[128,512]{1,0:T(8,128)}, /*index=5*/f32[128,512]{1,0...) while((s32[]{:T(128)}, f32[32,64,256]{2,1,0:T(8,128)S(1)}, ...), condition=%wide.region_12.16_spmd.clone.clone, body=%wide.region_10.0_spmd.clone.clone.sunk | while | flops 406722656 | bytes 12264079 | solution.py:71
  608.0 11.7 %cholesky.164 = f32[128,128]{1,0:T(8,128)S(1)} custom-call(f32[128,128]{1,0:T(8,128)S(1)} %cholesky.197), custom_call_target="Cholesky" | custom-call | tf_op jit(solution)/shard_map/jit(cholesky)/cholesky | solution.py:12
  619.7 9.8 %custom-call.22 = f32[1,128,128]{1,2,0:T(8,128)S(1)} custom-call(f32[1,128,128]{2,1,0:T(8,128)S(1)} %get-tuple-element.428), custom_call_target="InvertDiagBlocksLowerTriangular" | custom-call | tf_op jit(solution)/shard_map/jit(cholesky)/cholesky | solution.py:12
  630.0 11.7 %cholesky.181 = f32[128,128]{1,0:T(8,128)S(1)} custom-call(f32[128,128]{1,0:T(8,128)S(1)} %convolution_subtract_fusion.4), custom_call_target="Cholesky" | custom-call | tf_op jit(solution)/shard_map/jit(cholesky)/cholesky | solution.py:12
  644.3 4.1 while.35
  648.4 19.7 %custom-call.23 = f32[2,128,128]{1,2,0:T(8,128)S(1)} custom-call(f32[2,128,128]{2,1,0:T(8,128)S(1)} %get-tuple-element.321), custom_call_target="InvertDiagBlocksLowerTriangular" | custom-call | tf_op jit(solution)/shard_map/triangular_solve/custom-call.0 | solution.py:13
  668.1 148.2 %reduce-scatter.5.cloned.1.call-done = f32[256,256]{1,0:T(8,128)} async-done(((f32[2048,256]{1,0:T(8,128)}), f32[256,256]{1,0:T(8,128)}) %reduce-scatter.5.cloned.1.call-update) | async-done | bytes 262160 | tf_op jit(solution)/shard_map/reduce_scatter | solution.py:144
  820.1 12.7 %psum.30 = f32[256]{0:T(256)S(1)} all-reduce(f32[256]{0:T(256)S(1)} %multiply_reduce_fusion), channel_id=1, replica_groups=mesh['user'=8,'item'=16] {'user'}, use_global_device_ids=true, to_apply=%region_15.19 | all-reduce | flops 256 | bytes 2048 | tf_op jit(solution)/shard_map/psum | solution.py:80
  832.8 64.9 %psum.31 = f32[256]{0:T(256)S(1)} all-reduce(f32[256]{0:T(256)S(1)} %psum.30), channel_id=1, replica_groups=mesh['user'=8,'item'=16] {'item'}, use_global_device_ids=true, to_apply=%region_16.20 | all-reduce | flops 256 | bytes 2048 | tf_op jit(solution)/shard_map/psum | solution.py:81
  (193 shorter events, 148.5 us)
Async XLA Ops:
  8.0 28.5 %all-gather.3.cloned.1.call-start = ((), (), s32[]{:S(2)}) async-start(), calls=%async_computation.3 | async-start | bytes 1179648 | tf_op jit(solution)/shard_map/all_gather | solution.py:106
  9.7 149.5 %all-reduce.4.cloned.1.call-start = ((), (), s32[]{:S(2)}) async-start(), calls=%async_computation.2 | async-start | bytes 524288 | tf_op jit(solution)/shard_map/psum | solution.py:102
  12.1 334.9 %reduce-scatter.3.cloned.1.call-start = ((), (), s32[]{:S(2)}) async-start(), calls=%async_computation.4 | async-start | bytes 4456448 | tf_op jit(solution)/shard_map/reduce_scatter | solution.py:121
  14.8 24.1 %copy-start.4 = (s32[1,1,128]{2,1,0:T(1,128)S(1)}, s32[1,1,128]{2,1,0:T(1,128)}, u32[]{:S(2)}) copy-start(s32[1,1,128]{2,1,0:T(1,128)} %param.22) | copy-start | bytes 1540
  14.8 24.1 %copy-start.5 = (s32[1,1,128]{2,1,0:T(1,128)S(1)}, s32[1,1,128]{2,1,0:T(1,128)}, u32[]{:S(2)}) copy-start(s32[1,1,128]{2,1,0:T(1,128)} %param.20) | copy-start | bytes 1540
  14.8 24.1 %copy-start.6 = (s32[1,1,128]{2,1,0:T(1,128)S(1)}, s32[1,1,128]{2,1,0:T(1,128)}, u32[]{:S(2)}) copy-start(s32[1,1,128]{2,1,0:T(1,128)} %param.21) | copy-start | bytes 1540
  96.6 0.7 copy-start.3
  96.6 72.8 %copy-start.1 = (bf16[64,64,256]{2,1,0:T(8,128)(2,1)}, bf16[64,64,256]{2,1,0:T(8,128)(2,1)S(1)}, u32[]{:S(2)}) copy-start(bf16[64,64,256]{2,1,0:T(8,128)(2,1)S(1)} %get-tuple-element.818) | copy-start | bytes 6291460
  96.6 396.0 %all-reduce.6.cloned.1.call-start = ((), (), s32[]{:S(2)}) async-start(), calls=%async_computation.5 | async-start | bytes 524288 | tf_op jit(solution)/shard_map/psum | solution.py:123
  351.8 190.2 %all-gather.5.cloned.1.call-start = ((), (), s32[]{:S(2)}) async-start(), calls=%async_computation.6 | async-start | bytes 2228224 | tf_op jit(solution)/shard_map/all_gather | solution.py:129
  497.1 319.1 %reduce-scatter.5.cloned.1.call-start = ((), (), s32[]{:S(2)}) async-start(), calls=%async_computation.7 | async-start | bytes 2359296 | tf_op jit(solution)/shard_map/reduce_scatter | solution.py:144
  546.4 60.5 %copy-start.2 = (f32[256,256]{0,1:T(8,128)S(1)}, f32[256,256]{0,1:T(8,128)}, u32[]{:S(2)}) copy-start(f32[256,256]{0,1:T(8,128)} %get-tuple-element.409) | copy-start | bytes 786436
  605.5 1.4 copy-start
Sparse Core Ops, SparseCore 0:
  10.5 25.8 all-gather.2
  96.8 250.1 reduce-scatter.2
  497.2 44.7 all-gather.4
  607.0 209.1 reduce-scatter.4
Sparse Core Ops, SparseCore 1:
  14.9 144.3 all-reduce.3
  351.9 140.7 all-reduce.5
